TPU v7x, 256 devices: a whole 4x4x8 slice. The times are simulated.
256 devices in a mesh: dp: 16 (over z, y_lo), tensor: 4 (over x), section: 4 (over y_hi, core).
Axes of the slice: x: 4, y: 4 (y_hi: 2, y_lo: 2; y = y_hi * 2 + y_lo), z: 8, core: 2. Of those that a mesh axis runs over, the one named last changes fastest.
Arguments:
- grad_parts: bfloat16 [4, 16, 4, 1024, 1024], P('section', 'dp', None, None, 'tensor'), may hold values from -1.5 to 1.5
- first_moment: float32 [4, 4, 1024, 1024], P('section', 'tensor', 'dp'), may hold values from -3 to 3
- second_moment: float32 [4, 4, 1024, 1024], P('section', 'tensor', 'dp'), may hold values from 0.1 to 4
- left_stat: float32 [4, 4, 1024, 1024], P('section', 'tensor', 'dp'), may hold values from -12288 to 184320
- right_stat: float32 [4, 4, 1024, 1024], P('section', 'tensor', 'dp'), may hold values from -12288 to 184320
- left_basis: float32 [4, 4, 1024, 1024], P('section', 'tensor', 'dp'), may hold values from -0.1875 to 0.1875
- right_basis: float32 [4, 4, 1024, 1024], P('section', 'tensor', 'dp'), may hold values from -0.1875 to 0.1875
- gain_grads: float32 [4, 16, 4, 2, 1024], P('section', 'dp', 'tensor'), may hold values from -1.2 to 1.2
- gain_first: float32 [4, 2, 1024], P('section'), may hold values from -3 to 3
- gain_second: float32 [4, 2, 1024], P('section'), may hold values from 0.1 to 4
- table_grads: float32 [4, 16, 32, 16], P('section', 'dp', None, 'tensor'), may hold values from -1.2 to 1.2
- table_first: float32 [32, 16], P(None, 'tensor'), may hold values from -3 to 3
- table_second: float32 [32, 16], P(None, 'tensor'), may hold values from 0.1 to 4
Outputs:
- update: float32 [4, 4, 1024, 1024], P('section', 'tensor', 'dp')
- first_next: float32 [4, 4, 1024, 1024], P('section', 'tensor', 'dp')
- second_next: float32 [4, 4, 1024, 1024], P('section', 'tensor', 'dp')
- left_next: float32 [4, 4, 1024, 1024], P('section', 'tensor', 'dp')
- right_next: float32 [4, 4, 1024, 1024], P('section', 'tensor', 'dp')
- left_rotation: float32 [4, 4, 1024, 1024], P('section', 'tensor', 'dp')
- right_rotation: float32 [4, 4, 1024, 1024], P('section', 'tensor', 'dp')
- gain_update: float32 [4, 2, 1024], P('section')
- gain_moment: float32 [4, 2, 1024], P('section')
- gain_squares: float32 [4, 2, 1024], P('section')
- table_update: float32 [32, 16], P(None, 'tensor')
- table_moment: float32 [32, 16], P(None, 'tensor')
- table_squares: float32 [32, 16], P(None, 'tensor')
All inputs are finite; a program needn't handle non-finite values.
Results may differ from a plain program's by a relative error of at most 0.014.
Values may be sent and summed in bfloat16 or wider, within the bound.
A program may use at most 64 MiB of HBM per device.

v0:
```python
import jax
import jax.numpy as jnp
from jax import lax
from jax.sharding import PartitionSpec as P

NS_ITERS = 3
beta_first = 0.9
beta_second = 0.95
beta_stat = 0.95
adam_eps = 1e-08
norm_eps = 1e-06
step_count = 10.0


def to_half(value):
    return value.astype(jnp.bfloat16)


def batched(pattern, left, right):
    return jnp.einsum(pattern, left, right, preferred_element_type=jnp.float32)


def adam_direction(first, second):
    first_hat = first / (1.0 - beta_first**step_count)
    second_hat = second / (1.0 - beta_second**step_count)
    return first_hat / (jnp.sqrt(second_hat) + adam_eps)


def local(
    grad_parts,
    first_moment,
    second_moment,
    left_stat,
    right_stat,
    left_basis,
    right_basis,
    gain_grads,
    gain_first,
    gain_second,
    table_grads,
    table_first,
    table_second,
):
    partial_value = grad_parts[0, 0]
    columns = lax.all_to_all(partial_value, "tensor", split_axis=0, concat_axis=2, tiled=True)
    summed = lax.psum_scatter(
        columns.astype(jnp.float32).astype(jnp.bfloat16), "dp", scatter_dimension=1, tiled=True
    ).astype(jnp.float32)
    grad_rows = to_half(summed)
    row_count = grad_rows.shape[1]
    offset = lax.axis_index("dp") * row_count
    left_local = to_half(left_basis[0])
    right_local = to_half(right_basis[0])
    left_full, right_full = (
        lax.all_gather(left_local, "dp", axis=1, tiled=True),
        lax.all_gather(right_local, "dp", axis=1, tiled=True),
    )
    grad_full = lax.all_gather(grad_rows, "dp", axis=1, tiled=True)
    rotated_half = to_half(batched("mik,mkj->mij", grad_rows, right_full))
    block = left_local
    rotated = jnp.swapaxes(
        lax.psum_scatter(
            batched("mkc,mkj->cmj", block, rotated_half), "dp", scatter_dimension=0, tiled=True
        ),
        0,
        1,
    )
    first_new = beta_first * first_moment[0] + (1.0 - beta_first) * rotated
    second_new = beta_second * second_moment[0] + (1.0 - beta_second) * rotated * rotated
    direction = to_half(adam_direction(first_new, second_new))
    block = left_local
    back_half = to_half(
        batched("mik,mkj->mij", block, lax.all_gather(direction, "dp", axis=1, tiled=True))
    )
    update = batched("mik,mjk->mij", back_half, right_full)
    grad_columns = lax.dynamic_slice_in_dim(grad_full, offset, row_count, 2)
    left_new = beta_stat * left_stat[0] + batched("mik,mjk->mij", grad_rows, grad_full)
    right_new = beta_stat * right_stat[0] + batched("mki,mkj->mij", grad_columns, grad_full)
    power_left = batched("mik,mkj->mij", to_half(left_new), left_full)
    power_right = batched("mik,mkj->mij", to_half(right_new), right_full)
    power = jnp.concatenate([power_left, power_right], axis=0)
    squares = lax.psum(jnp.sum(power * power, axis=(1, 2)), "dp")
    iterate = power / jnp.sqrt(squares + norm_eps)[:, None, None]
    for sweep in range(NS_ITERS):
        iterate_half = to_half(iterate)
        iterate_full = lax.all_gather(iterate_half, "dp", axis=1, tiled=True)
        gram = to_half(batched("mik,mjk->mij", iterate_half, iterate_full))
        iterate = 1.5 * iterate - 0.5 * batched("mik,mkj->mij", gram, iterate_full)
    local_mats = power_left.shape[0]
    left_rotation = iterate[:local_mats]
    right_rotation = iterate[local_mats:]
    gain_sum = lax.psum(gain_grads[0, 0, 0], ("dp", "tensor"))
    gain_moment = beta_first * gain_first[0] + (1.0 - beta_first) * gain_sum
    gain_squares = beta_second * gain_second[0] + (1.0 - beta_second) * gain_sum * gain_sum
    gain_update = adam_direction(gain_moment, gain_squares)
    table_sum = lax.psum(table_grads[0, 0], ("dp", "section"))
    table_moment = beta_first * table_first + (1.0 - beta_first) * table_sum
    table_squares = beta_second * table_second + (1.0 - beta_second) * table_sum * table_sum
    table_update = adam_direction(table_moment, table_squares)
    return (
        update[None],
        first_new[None],
        second_new[None],
        left_new[None],
        right_new[None],
        left_rotation[None],
        right_rotation[None],
        gain_update[None],
        gain_moment[None],
        gain_squares[None],
        table_update,
        table_moment,
        table_squares,
    )


def solution(mesh):
    return jax.shard_map(
        local,
        mesh=mesh,
        in_specs=(
            P("section", "dp", None, None, "tensor"),
            P("section", "tensor", "dp", None),
            P("section", "tensor", "dp", None),
            P("section", "tensor", "dp", None),
            P("section", "tensor", "dp", None),
            P("section", "tensor", "dp", None),
            P("section", "tensor", "dp", None),
            P("section", "dp", "tensor", None, None),
            P("section", None, None),
            P("section", None, None),
            P("section", "dp", None, "tensor"),
            P(None, "tensor"),
            P(None, "tensor"),
        ),
        out_specs=(
            P("section", "tensor", "dp", None),
            P("section", "tensor", "dp", None),
            P("section", "tensor", "dp", None),
            P("section", "tensor", "dp", None),
            P("section", "tensor", "dp", None),
            P("section", "tensor", "dp", None),
            P("section", "tensor", "dp", None),
            P("section", None, None),
            P("section", None, None),
            P("section", None, None),
            P(None, "tensor"),
            P(None, "tensor"),
            P(None, "tensor"),
        ),
        check_vma=False,
    )
```

profile of v0, /device:TPU:2, one launch (start us, length us, event | category | flops | bytes accessed | tf_op | source)
XLA Modules:
  0.0 1098.2 jit_solution(950655685034763806)
XLA Ops:
  7.2 0.0 reduce-scatter.4.cloned.1.call-start
  7.2 4.0 copy.47
  11.2 29.7 %all_to_all.18 = bf16[4,1024,256]{1,2,0:T(8,128)(2,1)S(1)} all-to-all(bf16[4,1024,256]{1,2,0:T(8,128)(2,1)} %bitcast.140), channel_id=1, replica_groups=mesh['dp'=16,'tensor'=4,'section'=4] {'tensor'}, dimensions={0} | all-to-all | bytes 4194304 | tf_op jit(solution)/shard_map/all_to_all | solution.py:45
  40.9 7.8 copy.50
  48.7 4.4 copy.60
  53.0 0.0 reduce-scatter.4.cloned.1.call-update
  53.1 0.0 all-gather.12.cloned.1.call-start
  53.1 77.8 %reduce-scatter.4.cloned.1.call-done = bf16[64,1024]{1,0:T(8,128)(2,1)} async-done(((bf16[1024,1024]{1,0:T(8,128)(2,1)}), bf16[64,1024]{1,0:T(8,128)(2,1)}) %reduce-scatter.4.cloned.1.call-update) | async-done | bytes 131088
  130.9 1.0 reshape_bitcast_fusion
  132.0 0.7 copy.49
  132.7 0.0 all-gather.12.cloned.1.call-update
  132.7 0.0 all-gather.20.cloned.1.call-start
  132.8 0.7 convert_element_type.84
  133.4 0.0 all-gather.20.cloned.1.call-update
  133.5 0.0 all-gather.22.cloned.1.call-start
  133.5 0.7 convert_element_type.87
  134.2 0.0 all-gather.22.cloned.1.call-update
  134.2 0.0 all-gather.14.cloned.1.call-start
  134.3 0.2 copy.51
  134.5 0.0 copy-start.11
  134.5 70.3 %all-gather.12.cloned.1.call-done = bf16[1,1024,1024]{2,1,0:T(8,128)(2,1)} async-done(((bf16[1,64,1024]{2,1,0:T(8,128)(2,1)}), bf16[1,1024,1024]{2,1,0:T(8,128)(2,1)}) %all-gather.12.cloned.1.call-update) | async-done | bytes 2097168 | tf_op jit(solution)/shard_map/all_gather | solution.py:58
  204.7 2.5 fusion.20
  207.2 0.0 copy-start.6
  207.2 70.5 %all-gather.20.cloned.1.call-done = bf16[1,1,1024,1024]{3,2,1,0:T(8,128)(2,1)} async-done(((bf16[1,1,64,1024]{3,2,1,0:T(8,128)(2,1)}), bf16[1,1,1024,1024]{3,2,1,0:T(8,128)(2,1)}) %all-gather.20.cloned.1.call-update) | async-done | bytes 2097168 | tf_op jit(solution)/shard_map/all_gather | solution.py:56
  277.7 2.1 fusion.26
  279.8 0.8 fusion.17
  280.6 0.0 copy-start.7
  280.6 0.0 copy-start.3
  280.6 69.9 %all-gather.22.cloned.1.call-done = bf16[1,1,1024,1024]{3,2,1,0:T(8,128)(2,1)} async-done(((bf16[1,1,64,1024]{3,2,1,0:T(8,128)(2,1)}), bf16[1,1,1024,1024]{3,2,1,0:T(8,128)(2,1)}) %all-gather.22.cloned.1.call-update) | async-done | bytes 2097168 | tf_op jit(solution)/shard_map/all_gather | solution.py:55
  350.5 2.1 fusion.29
  352.6 0.2 multiply_reduce_fusion
  352.8 32.8 %psum.21 = f32[2]{0:T(128)S(1)} all-reduce(f32[2]{0:T(128)S(1)} %multiply_reduce_fusion), channel_id=1, replica_groups=mesh['dp'=16,'tensor'=4,'section'=4] {'dp'}, use_global_device_ids=true, to_apply=%region_3.0 | all-reduce | flops 2 | bytes 16 | tf_op jit(solution)/shard_map/psum | solution.py:82
  385.6 0.8 fusion.68
  386.4 0.0 all-gather.14.cloned.1.call-update
  386.4 0.0 copy-done.7
  386.4 0.0 all-reduce.3.cloned.1.call-start
  386.5 3.2 convolution_bitcast_fusion
  389.7 11.0 %copy.48 = f32[1024,1,1024]{2,1,0:T(1,128)} copy(f32[1024,1,1024]{0,2,1:T(8,128)} %convolution_bitcast_fusion) | data formatting | bytes 8388608 | tf_op jit(solution)/shard_map/mkc,mkj->cmj/transpose | solution.py:20
  400.8 0.0 all-reduce.3.cloned.1.call-update
  400.8 0.0 copy-start.14
  400.8 0.0 copy-start.4
  400.8 0.0 copy-start.5
  400.8 0.0 all-gather.16.cloned.1.call-start
  400.9 84.0 %all-gather.14.cloned.1.call-done = bf16[2,1024,1024]{2,1,0:T(8,128)(2,1)} async-done(((bf16[2,64,1024]{2,1,0:T(8,128)(2,1)}), bf16[2,1024,1024]{2,1,0:T(8,128)(2,1)}) %all-gather.14.cloned.1.call-update) | async-done | bytes 4194320 | tf_op jit(solution)/shard_map/all_gather | solution.py:86
  484.9 6.5 fusion.73
  491.4 0.0 all-gather.16.cloned.1.call-update
  491.4 0.0 all-gather.10.cloned.1.call-start
  491.5 0.6 dynamic-slice
  492.7 193.9 %all-reduce.3.cloned.1.call-done = f32[1024,1,1024]{2,1,0:T(1,128)} async-done(((f32[1024,1,1024]{2,1,0:T(1,128)}), f32[1024,1,1024]{2,1,0:T(1,128)}) %all-reduce.3.cloned.1.call-update) | async-done | bytes 4194320
  686.6 1.0 constant_dynamic-slice_fusion
  687.6 0.8 fusion.57
  688.4 0.0 all-gather.10.cloned.1.call-update
  688.5 0.0 all-gather.18.cloned.1.call-start
  688.5 99.6 %all-gather.16.cloned.1.call-done = bf16[2,1024,1024]{2,1,0:T(8,128)(2,1)} async-done(((bf16[2,64,1024]{2,1,0:T(8,128)(2,1)}), bf16[2,1024,1024]{2,1,0:T(8,128)(2,1)}) %all-gather.16.cloned.1.call-update) | async-done | bytes 4194320 | tf_op jit(solution)/shard_map/all_gather | solution.py:86
  788.1 6.4 fusion.76
  794.6 0.0 all-gather.18.cloned.1.call-update
  794.6 128.0 %psum.23 = f32[32,4]{0,1:T(4,128)} all-reduce(f32[32,4]{0,1:T(4,128)S(1)} %bitcast.144), channel_id=1, replica_groups=mesh['dp'=16,'tensor'=4,'section'=4] {'dp','section'}, use_global_device_ids=true, to_apply=%region_5.0 | all-reduce | flops 128 | bytes 1024 | tf_op jit(solution)/shard_map/psum | solution.py:96
  922.6 155.6 %psum.22 = f32[2,1024]{1,0:T(2,128)S(1)} all-reduce(f32[2,1024]{1,0:T(2,128)S(1)} %bitcast.143), channel_id=1, replica_groups=mesh['dp'=16,'tensor'=4,'section'=4] {'dp','tensor'}, use_global_device_ids=true, to_apply=%region_4.0 | all-reduce | flops 2048 | bytes 16384 | tf_op jit(solution)/shard_map/psum | solution.py:92
  1078.2 1.3 add_divide_fusion.1
  1079.5 1.4 fusion.69
  1080.9 0.9 fusion.48
  1081.8 3.5 fusion.23
  1085.3 5.6 fusion.14
  1090.9 0.8 slice_bitcast_fusion
  (25 shorter events, 0.1 us)
Async XLA Ops:
  7.2 123.7 %reduce-scatter.4.cloned.1.call-start = ((), (), s32[]{:S(2)}) async-start(), calls=%async_computation.9 | async-start | bytes 2228224
  53.0 79.7 %copy-start.8 = (f32[1,1,64,1024]{3,2,1,0:T(8,128)S(1)}, f32[1,1,64,1024]{3,2,1,0:T(8,128)}, u32[]{:S(2)}) copy-start(f32[1,1,64,1024]{3,2,1,0:T(8,128)} %param.19) | copy-start | bytes 786436
  53.0 80.5 %copy-start.9 = (f32[1,1,64,1024]{3,2,1,0:T(8,128)S(1)}, f32[1,1,64,1024]{3,2,1,0:T(8,128)}, u32[]{:S(2)}) copy-start(f32[1,1,64,1024]{3,2,1,0:T(8,128)} %param.18) | copy-start | bytes 786436
  53.0 151.7 %copy-start.10 = (f32[1,1,64,1024]{3,2,1,0:T(8,128)S(1)}, f32[1,1,64,1024]{3,2,1,0:T(8,128)}, u32[]{:S(2)}) copy-start(f32[1,1,64,1024]{3,2,1,0:T(8,128)} %param.17) | copy-start | bytes 786436
  53.1 151.7 %all-gather.12.cloned.1.call-start = ((), (), s32[]{:S(2)}) async-start(), calls=%async_computation.3 | async-start | bytes 2228224 | tf_op jit(solution)/shard_map/all_gather | solution.py:58
  132.7 145.0 %all-gather.20.cloned.1.call-start = ((), (), s32[]{:S(2)}) async-start(), calls=%async_computation.7 | async-start | bytes 2228224 | tf_op jit(solution)/shard_map/all_gather | solution.py:56
  133.5 217.1 %all-gather.22.cloned.1.call-start = ((), (), s32[]{:S(2)}) async-start(), calls=%async_computation.8 | async-start | bytes 2228224 | tf_op jit(solution)/shard_map/all_gather | solution.py:55
  134.2 350.7 %all-gather.14.cloned.1.call-start = ((), (), s32[]{:S(2)}) async-start(), calls=%async_computation.4 | async-start | bytes 4456448 | tf_op jit(solution)/shard_map/all_gather | solution.py:86
  134.5 145.3 %copy-start.11 = (f32[1,1,64,1024]{3,2,1,0:T(8,128)S(1)}, f32[1,1,64,1024]{3,2,1,0:T(8,128)}, u32[]{:S(2)}) copy-start(f32[1,1,64,1024]{3,2,1,0:T(8,128)} %param.16) | copy-start | bytes 786436
  204.7 75.0 %copy-start.1 = (bf16[1,1024,1024]{2,1,0:T(8,128)(2,1)S(1)}, bf16[1,1024,1024]{2,1,0:T(8,128)(2,1)}, u32[]{:S(2)}) copy-start(bf16[1,1024,1024]{2,1,0:T(8,128)(2,1)} %all-gather.12.cloned.1.call-done) | copy-start | bytes 6291460
  207.2 73.4 %copy-start.6 = (f32[64,1024]{1,0:T(8,128)}, f32[64,1024]{1,0:T(8,128)S(1)}, u32[]{:S(2)}) copy-start(f32[64,1024]{1,0:T(8,128)S(1)} %fusion.20) | copy-start | bytes 786436
  280.6 105.9 %copy-start.7 = (f32[64,1024]{1,0:T(8,128)}, f32[64,1024]{1,0:T(8,128)S(1)}, u32[]{:S(2)}) copy-start(f32[64,1024]{1,0:T(8,128)S(1)} %fusion.17) | copy-start | bytes 786436
  280.6 105.9 %copy-start = (bf16[1,1,1024,1024]{3,2,1,0:T(8,128)(2,1)S(1)}, bf16[1,1,1024,1024]{3,2,1,0:T(8,128)(2,1)}, u32[]{:S(2)}) copy-start(bf16[1,1,1024,1024]{3,2,1,0:T(8,128)(2,1)} %all-gather.20.cloned.1.call-done) | copy-start | bytes 6291460
  280.6 105.9 %copy-start.3 = (bf16[1,1,64,1024]{3,2,1,0:T(8,128)(2,1)S(1)}, bf16[1,1,64,1024]{3,2,1,0:T(8,128)(2,1)}, u32[]{:S(2)}) copy-start(bf16[1,1,64,1024]{3,2,1,0:T(8,128)(2,1)} %convert_element_type.87) | copy-start | bytes 393220
  386.4 300.2 %all-reduce.3.cloned.1.call-start = ((), (), s32[]{:S(2)}) async-start(), calls=%async_computation.10 | async-start | bytes 8388608
  400.8 90.7 %copy-start.14 = (u32[256]{0:T(256)S(1)}, u32[256]{0:T(256)}, u32[]{:S(2)}) copy-start(u32[256]{0:T(256)} %constant.66) | copy-start | bytes 3076
  400.8 286.8 %copy-start.4 = (f32[1,1,64,1024]{3,2,1,0:T(8,128)S(1)}, f32[1,1,64,1024]{3,2,1,0:T(8,128)}, u32[]{:S(2)}) copy-start(f32[1,1,64,1024]{3,2,1,0:T(8,128)} %param.15) | copy-start | bytes 786436
  400.8 286.8 %copy-start.5 = (f32[1,1,64,1024]{3,2,1,0:T(8,128)S(1)}, f32[1,1,64,1024]{3,2,1,0:T(8,128)}, u32[]{:S(2)}) copy-start(f32[1,1,64,1024]{3,2,1,0:T(8,128)} %param.14) | copy-start | bytes 786436
  400.8 387.3 %all-gather.16.cloned.1.call-start = ((), (), s32[]{:S(2)}) async-start(), calls=%async_computation.5 | async-start | bytes 4456448 | tf_op jit(solution)/shard_map/all_gather | solution.py:86
  491.4 590.4 %all-gather.10.cloned.1.call-start = ((), (), s32[]{:S(2)}) async-start(), calls=%async_computation.2 | async-start | bytes 2228224 | tf_op jit(solution)/shard_map/all_gather | solution.py:73
  688.5 396.8 %all-gather.18.cloned.1.call-start = ((), (), s32[]{:S(2)}) async-start(), calls=%async_computation.6 | async-start | bytes 4456448 | tf_op jit(solution)/shard_map/all_gather | solution.py:86
  788.1 6.5 copy-start.13
  788.1 134.5 %copy-start.12 = (f32[1,1,1,2,1024]{4,3,2,1,0:T(2,128)S(1)}, f32[1,1,1,2,1024]{4,3,2,1,0:T(2,128)}, u32[]{:S(2)}) copy-start(f32[1,1,1,2,1024]{4,3,2,1,0:T(2,128)} %param.20) | copy-start | bytes 24580
  1081.8 3.5 copy-start.2
Sparse Core Ops, SparseCore 0:
  53.2 77.7 reduce-scatter.3
  133.3 71.4 all-gather.11
  207.1 70.5 all-gather.19
  279.9 70.5 all-gather.21
  386.5 98.3 all-gather.13
  487.4 199.1 all-reduce.2
  689.0 99.1 all-gather.15
  790.5 73.1 all-gather.9
  866.1 98.3 all-gather.17
where the time goes:
time: 1100 us
  waiting for transfers between devices  666 us (61%)
  blocking collectives  346 us (31%)
  matrix products  32.5 us (3%)
  local copies, waits for them, and re-layouts  31.6 us (3%)
  between operations  14.7 us (1%)
    unnamed x11, waiting for transfers between devices  272 us
    all_gather x3, waiting for transfers between devices, local(): iterate_full = lax.all_gather(iterate_half, 'dp', axis=1, tiled=True)  184 us
    psum x1, blocking collectives, local(): gain_sum = lax.psum(gain_grads[0, 0, 0], ('dp', 'tensor'))  156 us
    psum x1, blocking collectives, local(): table_sum = lax.psum(table_grads[0, 0], ('dp', 'section'))  128 us
    all_gather x1, waiting for transfers between devices, local(): lax.all_gather(right_local, 'dp', axis=1, tiled=True)  70.5 us
    all_gather x1, waiting for transfers between devices, local(): grad_full = lax.all_gather(grad_rows, 'dp', axis=1, tiled=True)  70.3 us
    all_gather x1, waiting for transfers between devices, local(): lax.all_gather(left_local, 'dp', axis=1, tiled=True)  69.9 us
    psum x1, blocking collectives, local(): squares = lax.psum(jnp.sum(power * power, axis=(1, 2)), 'dp')  32.8 us
  transfers between devices with their start and end apart: 9, of which 7 were waited for; matrix products, arithmetic and copies ran while one was open for 4% of the time, Pallas kernels for 0%

commit v1 on v0

--- a/solution.py
+++ b/solution.py
@@ -42,7 +42,12 @@
     table_second,
 ):
     partial_value = grad_parts[0, 0]
-    columns = lax.all_to_all(partial_value, "tensor", split_axis=0, concat_axis=2, tiled=True)
+    columns = jnp.concatenate(
+        lax.all_to_all(
+            jnp.stack(jnp.split(partial_value, lax.axis_size("tensor"), axis=0)), "tensor", 0, 0
+        ),
+        axis=2,
+    )
     summed = lax.psum_scatter(
         columns.astype(jnp.float32).astype(jnp.bfloat16), "dp", scatter_dimension=1, tiled=True
     ).astype(jnp.float32)

time: 1100 us -> 1100 us (level)
  no operation moved by 1% of the time
where the time goes in v1:
time: 1100 us
  waiting for transfers between devices  666 us (61%)
  blocking collectives  346 us (31%)
  matrix products  32.5 us (3%)
  local copies, waits for them, and re-layouts  30 us (3%)
  between operations  14.8 us (1%)
    unnamed x11, waiting for transfers between devices  272 us
    all_gather x3, waiting for transfers between devices, local(): iterate_full = lax.all_gather(iterate_half, 'dp', axis=1, tiled=True)  184 us
    psum x1, blocking collectives, local(): gain_sum = lax.psum(gain_grads[0, 0, 0], ('dp', 'tensor'))  156 us
    psum x1, blocking collectives, local(): table_sum = lax.psum(table_grads[0, 0], ('dp', 'section'))  128 us
    all_gather x1, waiting for transfers between devices, local(): lax.all_gather(right_local, 'dp', axis=1, tiled=True)  70.5 us
    all_gather x1, waiting for transfers between devices, local(): grad_full = lax.all_gather(grad_rows, 'dp', axis=1, tiled=True)  70 us
    all_gather x1, waiting for transfers between devices, local(): lax.all_gather(left_local, 'dp', axis=1, tiled=True)  69.9 us
    psum x1, blocking collectives, local(): squares = lax.psum(jnp.sum(power * power, axis=(1, 2)), 'dp')  32.8 us
  transfers between devices with their start and end apart: 9, of which 7 were waited for; matrix products, arithmetic and copies ran while one was open for 4% of the time, Pallas kernels for 0%

profile of v1, /device:TPU:2, one launch (start us, length us, event | category | flops | bytes accessed | tf_op | source)
XLA Modules:
  0.0 1096.9 jit_solution(15400173710593928697)
XLA Ops:
  7.2 0.0 reduce-scatter.4.cloned.1.call-start
  7.2 1.7 fusion.73
  8.9 0.2 copy.66
  9.1 0.2 copy.65
  9.3 0.2 copy.64
  9.5 0.2 copy.63
  9.7 0.3 pad_maximum_fusion
  10.0 29.5 %all_to_all.5 = bf16[4,1,1024,256]{2,3,1,0:T(8,128)(2,1)S(1)} all-to-all(bf16[4,1,1024,256]{2,3,1,0:T(8,128)(2,1)S(1)} %pad_maximum_fusion), channel_id=1, replica_groups=mesh['dp'=16,'tensor'=4,'section'=4] {'tensor'}, dimensions={0} | all-to-all | bytes 4194304 | tf_op jit(solution)/shard_map/all_to_all | solution.py:46
  39.5 7.8 copy.57
  47.3 4.4 copy.71
  51.6 0.0 reduce-scatter.4.cloned.1.call-update
  51.7 0.0 all-gather.12.cloned.1.call-start
  51.7 78.0 %reduce-scatter.4.cloned.1.call-done = bf16[64,1024]{1,0:T(8,128)(2,1)} async-done(((bf16[1024,1024]{1,0:T(8,128)(2,1)}), bf16[64,1024]{1,0:T(8,128)(2,1)}) %reduce-scatter.4.cloned.1.call-update) | async-done | bytes 131088
  129.8 1.0 reshape_bitcast_fusion
  130.8 0.7 copy.56
  131.5 0.0 all-gather.12.cloned.1.call-update
  131.5 0.0 all-gather.20.cloned.1.call-start
  131.6 0.7 convert_element_type.84
  132.3 0.0 all-gather.20.cloned.1.call-update
  132.3 0.0 all-gather.22.cloned.1.call-start
  132.3 0.7 convert_element_type.87
  133.0 0.0 all-gather.22.cloned.1.call-update
  133.0 0.0 all-gather.14.cloned.1.call-start
  133.1 0.2 copy.58
  133.3 70.0 %all-gather.12.cloned.1.call-done = bf16[1,1024,1024]{2,1,0:T(8,128)(2,1)} async-done(((bf16[1,64,1024]{2,1,0:T(8,128)(2,1)}), bf16[1,1024,1024]{2,1,0:T(8,128)(2,1)}) %all-gather.12.cloned.1.call-update) | async-done | bytes 2097168 | tf_op jit(solution)/shard_map/all_gather | solution.py:63
  203.4 2.4 fusion.20
  205.8 0.0 copy-start.6
  205.8 70.5 %all-gather.20.cloned.1.call-done = bf16[1,1,1024,1024]{3,2,1,0:T(8,128)(2,1)} async-done(((bf16[1,1,64,1024]{3,2,1,0:T(8,128)(2,1)}), bf16[1,1,1024,1024]{3,2,1,0:T(8,128)(2,1)}) %all-gather.20.cloned.1.call-update) | async-done | bytes 2097168 | tf_op jit(solution)/shard_map/all_gather | solution.py:61
  276.3 2.1 fusion.26
  278.4 0.8 fusion.17
  279.2 0.0 copy-start.7
  279.2 69.9 %all-gather.22.cloned.1.call-done = bf16[1,1,1024,1024]{3,2,1,0:T(8,128)(2,1)} async-done(((bf16[1,1,64,1024]{3,2,1,0:T(8,128)(2,1)}), bf16[1,1,1024,1024]{3,2,1,0:T(8,128)(2,1)}) %all-gather.22.cloned.1.call-update) | async-done | bytes 2097168 | tf_op jit(solution)/shard_map/all_gather | solution.py:60
  349.1 2.1 fusion.29
  351.2 0.2 multiply_reduce_fusion
  351.4 32.8 %psum.21 = f32[2]{0:T(128)S(1)} all-reduce(f32[2]{0:T(128)S(1)} %multiply_reduce_fusion), channel_id=1, replica_groups=mesh['dp'=16,'tensor'=4,'section'=4] {'dp'}, use_global_device_ids=true, to_apply=%region_3.0 | all-reduce | flops 2 | bytes 16 | tf_op jit(solution)/shard_map/psum | solution.py:87
  384.2 0.8 fusion.68
  385.0 0.0 all-gather.14.cloned.1.call-update
  385.1 0.0 all-reduce.3.cloned.1.call-start
  385.1 3.2 convolution_bitcast_fusion
  388.3 11.0 %copy.55 = f32[1024,1,1024]{2,1,0:T(1,128)} copy(f32[1024,1,1024]{0,2,1:T(8,128)} %convolution_bitcast_fusion) | data formatting | bytes 8388608 | tf_op jit(solution)/shard_map/mkc,mkj->cmj/transpose | solution.py:20
  399.3 0.0 all-reduce.3.cloned.1.call-update
  399.3 0.0 copy-start.14
  399.4 0.0 all-gather.16.cloned.1.call-start
  399.4 84.1 %all-gather.14.cloned.1.call-done = bf16[2,1024,1024]{2,1,0:T(8,128)(2,1)} async-done(((bf16[2,64,1024]{2,1,0:T(8,128)(2,1)}), bf16[2,1024,1024]{2,1,0:T(8,128)(2,1)}) %all-gather.14.cloned.1.call-update) | async-done | bytes 4194320 | tf_op jit(solution)/shard_map/all_gather | solution.py:91
  483.5 6.5 fusion.74
  490.0 0.0 all-gather.16.cloned.1.call-update
  490.0 0.0 all-gather.10.cloned.1.call-start
  490.1 0.6 dynamic-slice
  491.3 193.9 %all-reduce.3.cloned.1.call-done = f32[1024,1,1024]{2,1,0:T(1,128)} async-done(((f32[1024,1,1024]{2,1,0:T(1,128)}), f32[1024,1,1024]{2,1,0:T(1,128)}) %all-reduce.3.cloned.1.call-update) | async-done | bytes 4194320
  685.2 1.0 constant_dynamic-slice_fusion
  686.2 0.8 fusion.57
  687.0 0.0 all-gather.10.cloned.1.call-update
  687.1 0.0 all-gather.18.cloned.1.call-start
  687.1 99.6 %all-gather.16.cloned.1.call-done = bf16[2,1024,1024]{2,1,0:T(8,128)(2,1)} async-done(((bf16[2,64,1024]{2,1,0:T(8,128)(2,1)}), bf16[2,1024,1024]{2,1,0:T(8,128)(2,1)}) %all-gather.16.cloned.1.call-update) | async-done | bytes 4194320 | tf_op jit(solution)/shard_map/all_gather | solution.py:91
  786.7 6.5 fusion.77
  793.2 0.0 all-gather.18.cloned.1.call-update
  793.2 127.8 %psum.23 = f32[32,4]{0,1:T(4,128)} all-reduce(f32[32,4]{0,1:T(4,128)S(1)} %bitcast.150), channel_id=1, replica_groups=mesh['dp'=16,'tensor'=4,'section'=4] {'dp','section'}, use_global_device_ids=true, to_apply=%region_5.0 | all-reduce | flops 128 | bytes 1024 | tf_op jit(solution)/shard_map/psum | solution.py:101
  921.1 155.8 %psum.22 = f32[2,1024]{1,0:T(2,128)S(1)} all-reduce(f32[2,1024]{1,0:T(2,128)S(1)} %bitcast.149), channel_id=1, replica_groups=mesh['dp'=16,'tensor'=4,'section'=4] {'dp','tensor'}, use_global_device_ids=true, to_apply=%region_4.0 | all-reduce | flops 2048 | bytes 16384 | tf_op jit(solution)/shard_map/psum | solution.py:97
  1076.8 1.3 add_divide_fusion.1
  1078.2 1.4 fusion.69
  1079.5 0.9 fusion.48
  1080.4 3.5 fusion.23
  1083.9 5.6 fusion.14
  1089.5 0.8 slice_bitcast_fusion
  (30 shorter events, 0.1 us)
Async XLA Ops:
  7.2 122.6 %reduce-scatter.4.cloned.1.call-start = ((), (), s32[]{:S(2)}) async-start(), calls=%async_computation.9 | async-start | bytes 2228224
  51.6 79.9 %copy-start.8 = (f32[1,1,64,1024]{3,2,1,0:T(8,128)S(1)}, f32[1,1,64,1024]{3,2,1,0:T(8,128)}, u32[]{:S(2)}) copy-start(f32[1,1,64,1024]{3,2,1,0:T(8,128)} %param.19) | copy-start | bytes 786436
  51.6 80.7 %copy-start.9 = (f32[1,1,64,1024]{3,2,1,0:T(8,128)S(1)}, f32[1,1,64,1024]{3,2,1,0:T(8,128)}, u32[]{:S(2)}) copy-start(f32[1,1,64,1024]{3,2,1,0:T(8,128)} %param.18) | copy-start | bytes 786436
  51.6 151.7 %copy-start.10 = (f32[1,1,64,1024]{3,2,1,0:T(8,128)S(1)}, f32[1,1,64,1024]{3,2,1,0:T(8,128)}, u32[]{:S(2)}) copy-start(f32[1,1,64,1024]{3,2,1,0:T(8,128)} %param.17) | copy-start | bytes 786436
  51.7 151.7 %all-gather.12.cloned.1.call-start = ((), (), s32[]{:S(2)}) async-start(), calls=%async_computation.3 | async-start | bytes 2228224 | tf_op jit(solution)/shard_map/all_gather | solution.py:63
  131.5 144.8 %all-gather.20.cloned.1.call-start = ((), (), s32[]{:S(2)}) async-start(), calls=%async_computation.7 | async-start | bytes 2228224 | tf_op jit(solution)/shard_map/all_gather | solution.py:61
  132.3 216.8 %all-gather.22.cloned.1.call-start = ((), (), s32[]{:S(2)}) async-start(), calls=%async_computation.8 | async-start | bytes 2228224 | tf_op jit(solution)/shard_map/all_gather | solution.py:60
  133.0 350.5 %all-gather.14.cloned.1.call-start = ((), (), s32[]{:S(2)}) async-start(), calls=%async_computation.4 | async-start | bytes 4456448 | tf_op jit(solution)/shard_map/all_gather | solution.py:91
  133.3 145.1 %copy-start.11 = (f32[1,1,64,1024]{3,2,1,0:T(8,128)S(1)}, f32[1,1,64,1024]{3,2,1,0:T(8,128)}, u32[]{:S(2)}) copy-start(f32[1,1,64,1024]{3,2,1,0:T(8,128)} %param.16) | copy-start | bytes 786436
  203.4 75.0 %copy-start.1 = (bf16[1,1024,1024]{2,1,0:T(8,128)(2,1)S(1)}, bf16[1,1024,1024]{2,1,0:T(8,128)(2,1)}, u32[]{:S(2)}) copy-start(bf16[1,1024,1024]{2,1,0:T(8,128)(2,1)} %all-gather.12.cloned.1.call-done) | copy-start | bytes 6291460
  205.8 73.4 %copy-start.6 = (f32[64,1024]{1,0:T(8,128)}, f32[64,1024]{1,0:T(8,128)S(1)}, u32[]{:S(2)}) copy-start(f32[64,1024]{1,0:T(8,128)S(1)} %fusion.20) | copy-start | bytes 786436
  279.2 105.9 %copy-start.7 = (f32[64,1024]{1,0:T(8,128)}, f32[64,1024]{1,0:T(8,128)S(1)}, u32[]{:S(2)}) copy-start(f32[64,1024]{1,0:T(8,128)S(1)} %fusion.17) | copy-start | bytes 786436
  279.2 105.9 %copy-start = (bf16[1,1,1024,1024]{3,2,1,0:T(8,128)(2,1)S(1)}, bf16[1,1,1024,1024]{3,2,1,0:T(8,128)(2,1)}, u32[]{:S(2)}) copy-start(bf16[1,1,1024,1024]{3,2,1,0:T(8,128)(2,1)} %all-gather.20.cloned.1.call-done) | copy-start | bytes 6291460
  279.2 105.9 %copy-start.3 = (bf16[1,1,64,1024]{3,2,1,0:T(8,128)(2,1)S(1)}, bf16[1,1,64,1024]{3,2,1,0:T(8,128)(2,1)}, u32[]{:S(2)}) copy-start(bf16[1,1,64,1024]{3,2,1,0:T(8,128)(2,1)} %convert_element_type.87) | copy-start | bytes 393220
  385.1 300.2 %all-reduce.3.cloned.1.call-start = ((), (), s32[]{:S(2)}) async-start(), calls=%async_computation.10 | async-start | bytes 8388608
  399.3 90.8 %copy-start.14 = (u32[256]{0:T(256)S(1)}, u32[256]{0:T(256)}, u32[]{:S(2)}) copy-start(u32[256]{0:T(256)} %constant.66) | copy-start | bytes 3076
  399.3 286.8 %copy-start.4 = (f32[1,1,64,1024]{3,2,1,0:T(8,128)S(1)}, f32[1,1,64,1024]{3,2,1,0:T(8,128)}, u32[]{:S(2)}) copy-start(f32[1,1,64,1024]{3,2,1,0:T(8,128)} %param.15) | copy-start | bytes 786436
  399.3 286.8 %copy-start.5 = (f32[1,1,64,1024]{3,2,1,0:T(8,128)S(1)}, f32[1,1,64,1024]{3,2,1,0:T(8,128)}, u32[]{:S(2)}) copy-start(f32[1,1,64,1024]{3,2,1,0:T(8,128)} %param.14) | copy-start | bytes 786436
  399.4 387.4 %all-gather.16.cloned.1.call-start = ((), (), s32[]{:S(2)}) async-start(), calls=%async_computation.5 | async-start | bytes 4456448 | tf_op jit(solution)/shard_map/all_gather | solution.py:91
  490.0 590.4 %all-gather.10.cloned.1.call-start = ((), (), s32[]{:S(2)}) async-start(), calls=%async_computation.2 | async-start | bytes 2228224 | tf_op jit(solution)/shard_map/all_gather | solution.py:78
  687.1 396.8 %all-gather.18.cloned.1.call-start = ((), (), s32[]{:S(2)}) async-start(), calls=%async_computation.6 | async-start | bytes 4456448 | tf_op jit(solution)/shard_map/all_gather | solution.py:91
  786.7 6.5 copy-start.13
  786.7 134.3 %copy-start.12 = (f32[1,1,1,2,1024]{4,3,2,1,0:T(2,128)S(1)}, f32[1,1,1,2,1024]{4,3,2,1,0:T(2,128)}, u32[]{:S(2)}) copy-start(f32[1,1,1,2,1024]{4,3,2,1,0:T(2,128)} %param.20) | copy-start | bytes 24580
  1080.4 3.5 copy-start.2
Sparse Core Ops, SparseCore 0:
  51.8 77.9 reduce-scatter.3
  132.1 71.1 all-gather.11
  205.7 70.5 all-gather.19
  278.5 70.5 all-gather.21
  385.2 98.2 all-gather.13
  486.0 199.1 all-reduce.2
  687.6 99.1 all-gather.15
  789.1 73.1 all-gather.9
  864.7 98.3 all-gather.17
